TPU v7x, 768 devices: a whole 4x8x12 slice. The times are simulated.
768 devices in a mesh: dp: 16 (over x, z_lo), ctx: 48 (over y, z_hi, core).
Axes of the slice: x: 4, y: 8, z: 12 (z_hi: 3, z_lo: 4; z = z_hi * 4 + z_lo), core: 2. Of those that a mesh axis runs over, the one named last changes fastest.
Arguments:
- query_rows: bfloat16 [16, 6144, 2048], P('dp', 'ctx'), may hold values from -6 to 6
- key_rows: bfloat16 [16, 6144, 512], P('dp', 'ctx'), may hold values from -6 to 6
- value_rows: bfloat16 [16, 6144, 512], P('dp', 'ctx'), may hold values from -6 to 6
- out_grad: bfloat16 [16, 6144, 2048], P('dp', 'ctx'), may hold values from -6 to 6
- segment_ids: int32 [16, 6144], P('dp', 'ctx'), may hold values from 0 to 47, never falling along the last dimension, each value on 1 to 256 neighbouring positions
- home_rows: int32 [16, 768], P('dp', 'ctx'), may hold values from 0 to 15, as said below
Outputs:
- routed: bfloat16 [16, 48, 16, 2, 8, 2048], P('dp', 'ctx')
- query_grad: bfloat16 [16, 6144, 2048], P('dp', 'ctx')
- key_grad: bfloat16 [16, 6144, 512], P('dp', 'ctx')
- value_grad: bfloat16 [16, 6144, 512], P('dp', 'ctx')
Inputs may be any that keep to these rules, and one draw needn't show every extreme that they name: `segment_ids`: ids never fall along a sequence; every document holds 1 to 256 tokens, and some document holds exactly 256. `home_rows`: among the 16 stretches of one block, at most 2 name the same dp row; in every block column some dp row is named by exactly 2 stretches of every dp row's block.
All inputs are finite; a program needn't handle non-finite values.
Results may differ from a plain program's by a relative error of at most 0.014.
Values may be sent and summed in bfloat16 or wider, within the bound.
A program may use at most 32 MiB of HBM per device.

v0:
```python
import math

import jax
import jax.numpy as jnp
from jax import lax
from jax.sharding import PartitionSpec as P

HEAD_DIM = 128
QHEADS = 16
KVHEADS = 4
SPAN = 2
GROUP = 4


def from_behind(value, axis, steps):
    count = lax.axis_size(axis)
    leading, last = (max(0, -steps), min(count, count - steps))
    return lax.ppermute(value, axis, [(source, source + steps) for source in range(leading, last)])


def forward_part(query_block, key_window, value_window, allowed):
    scaling = 1.0 / math.sqrt(HEAD_DIM)
    block_len = query_block.shape[0]
    window = key_window.shape[0]
    query_heads = query_block.reshape(block_len, KVHEADS, GROUP, HEAD_DIM)
    key_heads = key_window.reshape(window, KVHEADS, HEAD_DIM)
    value_heads = value_window.reshape(window, KVHEADS, HEAD_DIM)
    scores = (
        jnp.einsum("qkgd,nkd->kgqn", query_heads, key_heads, preferred_element_type=jnp.float32)
        * scaling
    )
    scores = jnp.where(allowed, scores, -jnp.inf)
    highest = jnp.max(scores, axis=-1, keepdims=True)
    exp_total = jnp.sum(jnp.exp(scores - highest), axis=-1, keepdims=True)
    log_total = highest + jnp.log(exp_total)
    weights = jnp.exp(scores - log_total)
    weights_low = weights.astype(jnp.bfloat16)
    attended = jnp.einsum(
        "kgqn,nkd->qkgd", weights_low, value_heads, preferred_element_type=jnp.float32
    )
    attended = attended.reshape(block_len, QHEADS * HEAD_DIM).astype(jnp.bfloat16)
    return (attended, weights, weights_low)


def backward_part(
    query_block, key_window, value_window, grad_block, attended, weights, weights_low
):
    scaling = 1.0 / math.sqrt(HEAD_DIM)
    block_len = query_block.shape[0]
    window = key_window.shape[0]
    query_heads = query_block.reshape(block_len, KVHEADS, GROUP, HEAD_DIM)
    key_heads = key_window.reshape(window, KVHEADS, HEAD_DIM)
    value_heads = value_window.reshape(window, KVHEADS, HEAD_DIM)
    grad_heads = grad_block.reshape(block_len, KVHEADS, GROUP, HEAD_DIM)
    attended_heads = attended.reshape(block_len, KVHEADS, GROUP, HEAD_DIM)
    row_delta = jnp.einsum(
        "qkgd,qkgd->kgq", grad_heads, attended_heads, preferred_element_type=jnp.float32
    )
    grad_weights = jnp.einsum(
        "qkgd,nkd->kgqn", grad_heads, value_heads, preferred_element_type=jnp.float32
    )
    grad_scores = (weights * (grad_weights - row_delta[..., None]) * scaling).astype(jnp.bfloat16)
    query_grad = jnp.einsum(
        "kgqn,nkd->qkgd", grad_scores, key_heads, preferred_element_type=jnp.float32
    )
    query_grad = query_grad.reshape(block_len, QHEADS * HEAD_DIM).astype(jnp.bfloat16)
    key_terms = jnp.einsum(
        "kgqn,qkgd->nkd", grad_scores, query_heads, preferred_element_type=jnp.float32
    )
    value_terms = jnp.einsum(
        "kgqn,qkgd->nkd", weights_low, grad_heads, preferred_element_type=jnp.float32
    )
    return (
        query_grad,
        key_terms.reshape(window, KVHEADS * HEAD_DIM),
        value_terms.reshape(window, KVHEADS * HEAD_DIM),
    )


def regroup(attended, home_ids):
    sources = lax.axis_size("dp")
    piece_count = home_ids.shape[0]
    capacity = max(2, 2 * piece_count // sources)
    piece_len = attended.shape[0] // piece_count
    flattened = attended.reshape(piece_count, piece_len * attended.shape[1])
    positions = jnp.arange(piece_count, dtype=jnp.int32)
    matching = (home_ids[:, None] == home_ids[None, :]) & (positions[None, :] < positions[:, None])
    slot_index = jnp.sum(matching.astype(jnp.int32), axis=1)
    select = (home_ids[None, None, :] == jnp.arange(sources, dtype=jnp.int32)[:, None, None]) & (
        slot_index[None, None, :] == jnp.arange(capacity, dtype=jnp.int32)[None, :, None]
    )
    select = select.reshape(sources * capacity, piece_count).astype(jnp.bfloat16)
    packed = jnp.dot(select, flattened, preferred_element_type=jnp.float32).astype(jnp.bfloat16)
    packed = packed.reshape(sources, capacity, piece_len * attended.shape[1])
    arrived = lax.all_to_all(packed, "dp", split_axis=0, concat_axis=0, tiled=True)
    return arrived.reshape(1, 1, sources, capacity, piece_len, attended.shape[1])


def on_device(query_rows, key_rows, value_rows, out_grad, segment_ids, home_rows):
    query_block = query_rows[0]
    key_block = key_rows[0]
    value_block = value_rows[0]
    grad_block = out_grad[0]
    seg_block = segment_ids[0].astype(jnp.bfloat16)
    home_ids = home_rows[0]
    block_len = query_block.shape[0]
    column = lax.axis_index("ctx")
    fetched = {}
    current = (key_block, value_block, seg_block)
    for distance in range(1, SPAN + 1):
        current = from_behind((current[0], current[1], current[2]), "ctx", 1)
        fetched[distance] = current
    ordered = [fetched[distance] for distance in range(SPAN, 0, -1)] + [
        (key_block, value_block, seg_block)
    ]
    key_window = jnp.concatenate([piece[0] for piece in ordered], axis=0)
    value_window = jnp.concatenate([piece[1] for piece in ordered], axis=0)
    seg_window = jnp.concatenate([piece[2] for piece in ordered], axis=0)
    window = key_window.shape[0]
    pos_query = column * block_len + jnp.arange(block_len, dtype=jnp.int32)
    pos_key = (column - SPAN) * block_len + jnp.arange(window, dtype=jnp.int32)
    allowed = (
        (seg_block[:, None] == seg_window[None, :])
        & (pos_key[None, :] <= pos_query[:, None])
        & (pos_key[None, :] >= 0)
    )
    attended, weights, weights_low = forward_part(query_block, key_window, value_window, allowed)
    query_grad, key_terms, value_terms = backward_part(
        query_block, key_window, value_window, grad_block, attended, weights, weights_low
    )
    routed = regroup(attended, home_ids)

    def term_rows(terms, distance):
        start = (SPAN - distance) * block_len
        return terms[start : start + block_len]

    carried = (term_rows(key_terms, SPAN), term_rows(value_terms, SPAN))
    for distance in range(SPAN - 1, -1, -1):
        moved = from_behind((carried[0], carried[1]), "ctx", -1)
        carried = (
            moved[0] + term_rows(key_terms, distance),
            moved[1] + term_rows(value_terms, distance),
        )
    key_total, value_total = carried
    return (
        routed,
        query_grad[None],
        key_total.astype(jnp.bfloat16)[None],
        value_total.astype(jnp.bfloat16)[None],
    )


def solution(mesh):
    placed = (
        P("dp", "ctx", None),
        P("dp", "ctx", None),
        P("dp", "ctx", None),
        P("dp", "ctx", None),
        P("dp", "ctx"),
        P("dp", "ctx"),
    )
    return jax.shard_map(
        on_device,
        mesh=mesh,
        in_specs=placed,
        out_specs=(
            P("dp", "ctx", None, None, None, None),
            P("dp", "ctx", None),
            P("dp", "ctx", None),
            P("dp", "ctx", None),
        ),
        check_vma=False,
    )
```

profile of v0, /device:TPU:163, one launch (start us, length us, event | category | flops | bytes accessed | tf_op | source)
XLA Modules:
  0.0 147.7 jit_solution(12164883073174971140)
XLA Ops:
  1.3 11.2 %collective-permute-start.2 = (bf16[128]{0:T(256)(128)(2,1)S(1)}, bf16[128]{0:T(256)(128)(2,1)S(1)}, u32[]{:S(2)}, u32[]{:S(2)}) collective-permute-start(bf16[128]{0:T(256)(128)(2,1)S(1)} %convert_bitcast_fusion), channel_id=1, source_target_pairs={{0,1},{1,2},{2,3},{3,4},{4,5},{5,6},{6,7},{7,8},{8,9},{9,10},{10,1... | collective-permute-start | bytes 776 | tf_op jit(solution)/shard_map/ppermute | solution.py:18
  12.5 1.0 copy.33
  13.5 1.9 %collective-permute-start.4 = (bf16[128,512]{0,1:T(8,128)(2,1)S(1)}, bf16[128,512]{0,1:T(8,128)(2,1)S(1)}, u32[]{:S(2)}, u32[]{:S(2)}) collective-permute-start(bf16[128,512]{0,1:T(8,128)(2,1)S(1)} %bitcast.106), channel_id=1, source_target_pairs={{0,1},{1,2},{2,3},{3,4},{4,5},{5,6},{6,7},{7,8},{8,9},{9,10},{10,1... | collective-permute-start | bytes 393224 | tf_op jit(solution)/shard_map/ppermute | solution.py:18
  15.4 6.8 %collective-permute-start = (bf16[128,512]{1,0:T(8,128)(2,1)}, bf16[128,512]{1,0:T(8,128)(2,1)}, u32[]{:S(2)}, u32[]{:S(2)}) collective-permute-start(bf16[128,512]{1,0:T(8,128)(2,1)} %bitcast.108), channel_id=1, source_target_pairs={{0,1},{1,2},{2,3},{3,4},{4,5},{5,6},{6,7},{7,8},{8,9},{9,10},{10,1... | collective-permute-start | bytes 393224 | tf_op jit(solution)/shard_map/ppermute | solution.py:18
  23.9 1.7 %copy.32 = bf16[1,128,512]{1,2,0:T(8,128)(2,1)} copy(bf16[1,128,512]{2,1,0:T(8,128)(2,1)} %param.8) | data formatting | bytes 262144 | tf_op args[2]
  25.6 1.9 %collective-permute-start.3 = (bf16[128]{0:T(256)(128)(2,1)S(1)}, bf16[128]{0:T(256)(128)(2,1)S(1)}, u32[]{:S(2)}, u32[]{:S(2)}) collective-permute-start(bf16[128]{0:T(256)(128)(2,1)S(1)} %collective-permute-done.2), channel_id=1, source_target_pairs={{0,1},{1,2},{2,3},{3,4},{4,5},{5,6},{6,7},{7,8},{8,9},{9,10},{10,1... | collective-permute-start | bytes 776 | tf_op jit(solution)/shard_map/ppermute | solution.py:18
  27.7 2.0 %copy.77 = bf16[1,128,2048]{1,2,0:T(8,128)(2,1)} copy(bf16[1,128,2048]{2,1,0:T(8,128)(2,1)} %param.6) | data formatting | bytes 1048576 | tf_op jit(solution)/shard_map/reshape;squeeze | solution.py:25
  29.8 6.6 %collective-permute-start.5 = (bf16[128,512]{0,1:T(8,128)(2,1)S(1)}, bf16[128,512]{0,1:T(8,128)(2,1)S(1)}, u32[]{:S(2)}, u32[]{:S(2)}) collective-permute-start(bf16[128,512]{0,1:T(8,128)(2,1)S(1)} %collective-permute-done.4), channel_id=1, source_target_pairs={{0,1},{1,2},{2,3},{3,4},{4,5},{5,6},{6,7},{7,8},{8,9},{9,10},{10,1... | collective-permute-start | bytes 393224 | tf_op jit(solution)/shard_map/ppermute | solution.py:18
  37.4 1.9 %collective-permute-start.1 = (bf16[128,512]{1,0:T(8,128)(2,1)}, bf16[128,512]{1,0:T(8,128)(2,1)}, u32[]{:S(2)}, u32[]{:S(2)}) collective-permute-start(bf16[128,512]{1,0:T(8,128)(2,1)} %collective-permute-done), channel_id=1, source_target_pairs={{0,1},{1,2},{2,3},{3,4},{4,5},{5,6},{6,7},{7,8},{8,9},{9,10},{10,1... | collective-permute-start | bytes 393224 | tf_op jit(solution)/shard_map/ppermute | solution.py:18
  39.3 1.7 %copy.31 = bf16[128,512]{0,1:T(8,128)(2,1)} copy(bf16[128,512]{1,0:T(8,128)(2,1)} %collective-permute-done) | data formatting | bytes 262144 | tf_op jit(solution)/shard_map/ppermute | solution.py:18
  41.1 1.7 %fusion.4 = (f32[4,4,128]{2,1,0:T(4,128)S(1)}, f32[4,384,128,4]{2,1,3,0:T(8,128)S(1)}) fusion(pred[128,384]{0,1:T(8,128)(4,1)} %and_and_fusion, bf16[128,4,4,128]{0,3,2,1:T(8,128)(2,1)} %bitcast.97, bf16[128,4,128]{2,0,1:T(8,128)(2,1)S(1)} %copy.37, bf16[128,4,128]{2,0,1:T(8,128)(2,1)S(1)} %copy.36, bf16[128,4,128]{2,0,1:T(8,128)(2,1)S(1)} %copy.35), kind=kOutput, calls=%fused_computation.9 | convolution fusion | flops 204863488 | bytes 4120576 | tf_op jit(solution)/shard_map/qkgd,nkd->kgqn/dot_general | solution.py:29
  43.5 1.6 %collective-permute-done.1 = bf16[128,512]{1,0:T(8,128)(2,1)} collective-permute-done((bf16[128,512]{1,0:T(8,128)(2,1)}, bf16[128,512]{1,0:T(8,128)(2,1)}, u32[]{:S(2)}, u32[]{:S(2)}) %collective-permute-start.1) | collective-permute-done | bytes 131104 | tf_op jit(solution)/shard_map/ppermute | solution.py:18
  46.2 3.1 %bitcast_convert_fusion = (f32[4,4,128,128]{2,3,1,0:T(8,128)}, bf16[4,128,4,128]{3,1,2,0:T(8,128)(2,1)}) fusion(f32[4,384,128,4]{2,1,3,0:T(8,128)S(1)} %get-tuple-element.19, f32[4,4,128]{2,1,0:T(4,128)S(1)} %bitcast.119, pred[128,384]{0,1:T(8,128)(4,1)} %and_and_fusion, bf16[128,4,128]{0,2,1:T(8,128)(2,1)} %bitcast.109, ...), kind=kOutput, calls=%fused_computation.15 | convolution fusion | flops 206176256 | bytes 5169152 | tf_op jit(solution)/shard_map/kgqn,nkd->qkgd/dot_general | solution.py:38
  49.3 1.5 copy.40
  51.6 1.5 %reshape.142 = bf16[16,2,16384]{2,1,0:T(2,128)(2,1)} reshape(bf16[32,16384]{1,0:T(8,128)(2,1)S(1)} %convolution_convert_fusion) | data formatting | bytes 2097152 | tf_op jit(solution)/shard_map/reshape | solution.py:94
  53.1 10.7 %all-to-all-start = ((bf16[16,2,16384]{2,1,0:T(2,128)(2,1)}), bf16[16,2,16384]{2,1,0:T(2,128)(2,1)S(1)}, u32[]{:S(2)}, u32[]{:S(2)}) async-start(bf16[16,2,16384]{2,1,0:T(2,128)(2,1)} %reshape.142), calls=%async_computation | async-start | bytes 2097152 | tf_op jit(solution)/shard_map/all_to_all | solution.py:95
  65.4 2.8 %convolution_bitcast_fusion = f32[384,4,128]{0,2,1:T(8,128)S(1)} fusion(bf16[128,4,4,128]{0,3,2,1:T(8,128)(2,1)S(1)} %copy.51, f32[4,384,128,4]{2,1,3,0:T(8,128)} %copy-done, f32[4,4,128]{2,1,0:T(4,128)S(1)} %bitcast.120, pred[128,384]{0,1:T(8,128)(4,1)S(1)} %copy-done.8), kind=kOutput, calls=%fused_computation.10 | convolution fusion | flops 204472320 | bytes 4513792 | tf_op jit(solution)/shard_map/kgqn,qkgd->nkd/dot_general | solution.py:70
  69.8 6.5 %collective-permute-start.8 = (f32[128,512]{1,0:T(8,128)}, f32[128,512]{1,0:T(8,128)}, u32[]{:S(2)}, u32[]{:S(2)}) collective-permute-start(f32[128,512]{1,0:T(8,128)} %copy.52), channel_id=1, source_target_pairs={{1,0},{2,1},{3,2},{4,3},{5,4},{6,5},{7,6},{8,7},{9,8},{10,9},{11,1... | collective-permute-start | bytes 786440 | tf_op jit(solution)/shard_map/ppermute | solution.py:18
  76.3 1.8 %copy.65 = f32[4,4,128,128]{3,1,0,2:T(4,128)S(1)} copy(f32[4,4,128,128]{2,3,1,0:T(8,128)} %get-tuple-element.20) | data formatting | bytes 2097152
  79.1 3.4 %fusion.2 = bf16[4,4,128,384]{2,3,1,0:T(8,128)(2,1)S(1)} fusion(f32[4,384,128,4]{2,1,3,0:T(8,128)} %copy-done, bf16[128,4,4,128]{0,3,2,1:T(8,128)(2,1)} %copy-done.6, f32[4,4,128]{2,1,0:T(4,128)S(1)} %copy.66, f32[4,4,128]{2,1,0:T(4,128)S(1)} %bitcast.121, pred[128,384]{0,1:T(8,128)(4,1)S(1)} %copy-done.8, bf16[128,4,128]{0,2,1:T(8,128)(2,1)S(1)} %bitcast.110, ...), kind=kOutput, calls=%fused_computation.4 | convolution fusion | flops 208011264 | bytes 5701632 | tf_op jit(solution)/shard_map/qkgd,nkd->kgqn/dot_general | solution.py:59
  84.9 1.9 %collective-permute-start.6 = (f32[128,512]{1,0:T(8,128)}, f32[128,512]{1,0:T(8,128)}, u32[]{:S(2)}, u32[]{:S(2)}) collective-permute-start(f32[128,512]{1,0:T(8,128)} %copy.47), channel_id=1, source_target_pairs={{1,0},{2,1},{3,2},{4,3},{5,4},{6,5},{7,6},{8,7},{9,8},{10,9},{11,1... | collective-permute-start | bytes 786440 | tf_op jit(solution)/shard_map/ppermute | solution.py:18
  87.0 1.1 copy.48
  88.1 36.3 %collective-permute-done.8 = f32[128,512]{1,0:T(8,128)} collective-permute-done((f32[128,512]{1,0:T(8,128)}, f32[128,512]{1,0:T(8,128)}, u32[]{:S(2)}, u32[]{:S(2)}) %collective-permute-start.8) | collective-permute-done | bytes 262176 | tf_op jit(solution)/shard_map/ppermute | solution.py:18
  124.4 1.7 %add.51 = f32[128,512]{1,0:T(8,128)} add(f32[128,512]{1,0:T(8,128)} %collective-permute-done.8, f32[128,512]{1,0:T(8,128)S(1)} %copy.53) | non-fusion elementwise | flops 65536 | bytes 786432 | tf_op jit(solution)/shard_map/add | solution.py:142
  126.0 1.9 %collective-permute-start.9 = (f32[128,512]{1,0:T(8,128)}, f32[128,512]{1,0:T(8,128)}, u32[]{:S(2)}, u32[]{:S(2)}) collective-permute-start(f32[128,512]{1,0:T(8,128)} %add.51), channel_id=1, source_target_pairs={{1,0},{2,1},{3,2},{4,3},{5,4},{6,5},{7,6},{8,7},{9,8},{10,9},{11,1... | collective-permute-start | bytes 786440 | tf_op jit(solution)/shard_map/ppermute | solution.py:18
  128.0 1.7 %add.49 = f32[128,512]{1,0:T(8,128)} add(f32[128,512]{1,0:T(8,128)} %collective-permute-done.6, f32[128,512]{1,0:T(8,128)S(1)} %copy.48) | non-fusion elementwise | flops 65536 | bytes 786432 | tf_op jit(solution)/shard_map/add | solution.py:141
  129.7 9.5 %collective-permute-start.7 = (f32[128,512]{1,0:T(8,128)}, f32[128,512]{1,0:T(8,128)}, u32[]{:S(2)}, u32[]{:S(2)}) collective-permute-start(f32[128,512]{1,0:T(8,128)} %add.49), channel_id=1, source_target_pairs={{1,0},{2,1},{3,2},{4,3},{5,4},{6,5},{7,6},{8,7},{9,8},{10,9},{11,1... | collective-permute-start | bytes 786440 | tf_op jit(solution)/shard_map/ppermute | solution.py:18
  139.1 1.5 convolution_convert_fusion.1
  140.7 1.1 copy.49
  142.8 1.6 %fusion.7 = bf16[1,128,512]{2,1,0:T(8,128)(2,1)} fusion(f32[128,512]{1,0:T(8,128)} %collective-permute-done.9, f32[128,512]{1,0:T(8,128)S(1)} %copy.54), kind=kLoop, calls=%fused_computation.23 | loop fusion | flops 131072 | bytes 655360 | tf_op jit(solution)/shard_map/broadcast_in_dim | solution.py:149
  144.5 1.6 %fusion.6 = bf16[1,128,512]{2,1,0:T(8,128)(2,1)} fusion(f32[128,512]{1,0:T(8,128)} %collective-permute-done.7, f32[128,512]{1,0:T(8,128)S(1)} %copy.49), kind=kLoop, calls=%fused_computation.22 | loop fusion | flops 131072 | bytes 655360 | tf_op jit(solution)/shard_map/broadcast_in_dim | solution.py:148
  146.1 1.6 %reshape.143 = bf16[1,1,16,2,8,2048]{5,4,3,2,1,0:T(8,128)(2,1)} reshape(bf16[16,2,16384]{2,1,0:T(2,128)(2,1)S(1)} %all-to-all-done) | data formatting | bytes 2097152 | tf_op jit(solution)/shard_map/reshape | solution.py:96
  (62 shorter events, 13.8 us)
Async XLA Ops:
  1.3 24.3 %collective-permute-start.2 = (bf16[128]{0:T(256)(128)(2,1)S(1)}, bf16[128]{0:T(256)(128)(2,1)S(1)}, u32[]{:S(2)}, u32[]{:S(2)}) collective-permute-start(bf16[128]{0:T(256)(128)(2,1)S(1)} %convert_bitcast_fusion), channel_id=1, source_target_pairs={{0,1},{1,2},{2,3},{3,4},{4,5},{5,6},{6,7},{7,8},{8,9},{9,10},{10,1... | collective-permute-start | bytes 776 | tf_op jit(solution)/shard_map/ppermute | solution.py:18
  13.5 16.2 %collective-permute-start.4 = (bf16[128,512]{0,1:T(8,128)(2,1)S(1)}, bf16[128,512]{0,1:T(8,128)(2,1)S(1)}, u32[]{:S(2)}, u32[]{:S(2)}) collective-permute-start(bf16[128,512]{0,1:T(8,128)(2,1)S(1)} %bitcast.106), channel_id=1, source_target_pairs={{0,1},{1,2},{2,3},{3,4},{4,5},{5,6},{6,7},{7,8},{8,9},{9,10},{10,1... | collective-permute-start | bytes 393224 | tf_op jit(solution)/shard_map/ppermute | solution.py:18
  15.4 21.9 %collective-permute-start = (bf16[128,512]{1,0:T(8,128)(2,1)}, bf16[128,512]{1,0:T(8,128)(2,1)}, u32[]{:S(2)}, u32[]{:S(2)}) collective-permute-start(bf16[128,512]{1,0:T(8,128)(2,1)} %bitcast.108), channel_id=1, source_target_pairs={{0,1},{1,2},{2,3},{3,4},{4,5},{5,6},{6,7},{7,8},{8,9},{9,10},{10,1... | collective-permute-start | bytes 393224 | tf_op jit(solution)/shard_map/ppermute | solution.py:18
  25.6 4.1 %collective-permute-start.3 = (bf16[128]{0:T(256)(128)(2,1)S(1)}, bf16[128]{0:T(256)(128)(2,1)S(1)}, u32[]{:S(2)}, u32[]{:S(2)}) collective-permute-start(bf16[128]{0:T(256)(128)(2,1)S(1)} %collective-permute-done.2), channel_id=1, source_target_pairs={{0,1},{1,2},{2,3},{3,4},{4,5},{5,6},{6,7},{7,8},{8,9},{9,10},{10,1... | collective-permute-start | bytes 776 | tf_op jit(solution)/shard_map/ppermute | solution.py:18
  29.8 11.2 %collective-permute-start.5 = (bf16[128,512]{0,1:T(8,128)(2,1)S(1)}, bf16[128,512]{0,1:T(8,128)(2,1)S(1)}, u32[]{:S(2)}, u32[]{:S(2)}) collective-permute-start(bf16[128,512]{0,1:T(8,128)(2,1)S(1)} %collective-permute-done.4), channel_id=1, source_target_pairs={{0,1},{1,2},{2,3},{3,4},{4,5},{5,6},{6,7},{7,8},{8,9},{9,10},{10,1... | collective-permute-start | bytes 393224 | tf_op jit(solution)/shard_map/ppermute | solution.py:18
  37.4 6.1 %copy-start.3 = (bf16[128,4,128]{2,0,1:T(8,128)(2,1)}, bf16[128,4,128]{2,0,1:T(8,128)(2,1)S(1)}, u32[]{:S(2)}) copy-start(bf16[128,4,128]{2,0,1:T(8,128)(2,1)S(1)} %copy.36) | copy-start | bytes 393220
  37.4 7.8 %collective-permute-start.1 = (bf16[128,512]{1,0:T(8,128)(2,1)}, bf16[128,512]{1,0:T(8,128)(2,1)}, u32[]{:S(2)}, u32[]{:S(2)}) collective-permute-start(bf16[128,512]{1,0:T(8,128)(2,1)} %collective-permute-done), channel_id=1, source_target_pairs={{0,1},{1,2},{2,3},{3,4},{4,5},{5,6},{6,7},{7,8},{8,9},{9,10},{10,1... | collective-permute-start | bytes 393224 | tf_op jit(solution)/shard_map/ppermute | solution.py:18
  41.1 2.4 %copy-start.4 = (bf16[128,4,128]{2,0,1:T(8,128)(2,1)}, bf16[128,4,128]{2,0,1:T(8,128)(2,1)S(1)}, u32[]{:S(2)}) copy-start(bf16[128,4,128]{2,0,1:T(8,128)(2,1)S(1)} %copy.35) | copy-start | bytes 393220
  41.1 1.7 %copy-start.7 = (pred[128,384]{0,1:T(8,128)(4,1)S(1)}, pred[128,384]{0,1:T(8,128)(4,1)}, u32[]{:S(2)}) copy-start(pred[128,384]{0,1:T(8,128)(4,1)} %and_and_fusion) | copy-start | bytes 147460
  42.8 6.5 %copy-start = (f32[4,384,128,4]{2,1,3,0:T(8,128)}, f32[4,384,128,4]{2,1,3,0:T(8,128)S(1)}, u32[]{:S(2)}) copy-start(f32[4,384,128,4]{2,1,3,0:T(8,128)S(1)} %get-tuple-element.19) | copy-start | bytes 9437188
  46.2 4.6 %copy-start.10 = (bf16[128,512]{0,1:T(8,128)(2,1)}, bf16[128,512]{0,1:T(8,128)(2,1)S(1)}, u32[]{:S(2)}) copy-start(bf16[128,512]{0,1:T(8,128)(2,1)S(1)} %copy.30) | copy-start | bytes 393220
  51.2 12.6 %copy-start.5 = (bf16[1,128,2048]{2,1,0:T(8,128)(2,1)S(1)}, bf16[1,128,2048]{2,1,0:T(8,128)(2,1)}, u32[]{:S(2)}) copy-start(bf16[1,128,2048]{2,1,0:T(8,128)(2,1)} %param.9) | copy-start | bytes 1572868
  51.6 13.9 %copy-start.8 = (pred[128,384]{0,1:T(8,128)(4,1)S(1)}, pred[128,384]{0,1:T(8,128)(4,1)}, u32[]{:S(2)}) copy-start(pred[128,384]{0,1:T(8,128)(4,1)} %and_and_fusion) | copy-start | bytes 147460
  53.1 93.1 %all-to-all-start = ((bf16[16,2,16384]{2,1,0:T(2,128)(2,1)}), bf16[16,2,16384]{2,1,0:T(2,128)(2,1)S(1)}, u32[]{:S(2)}, u32[]{:S(2)}) async-start(bf16[16,2,16384]{2,1,0:T(2,128)(2,1)} %reshape.142), calls=%async_computation | async-start | bytes 2097152 | tf_op jit(solution)/shard_map/all_to_all | solution.py:95
  64.6 0.8 copy-start.6
  68.2 10.9 %copy-start.9 = (bf16[1,128,512]{1,2,0:T(8,128)(2,1)S(1)}, bf16[1,128,512]{1,2,0:T(8,128)(2,1)}, u32[]{:S(2)}) copy-start(bf16[1,128,512]{1,2,0:T(8,128)(2,1)} %copy.32) | copy-start | bytes 393220
  69.8 54.5 %collective-permute-start.8 = (f32[128,512]{1,0:T(8,128)}, f32[128,512]{1,0:T(8,128)}, u32[]{:S(2)}, u32[]{:S(2)}) collective-permute-start(f32[128,512]{1,0:T(8,128)} %copy.52), channel_id=1, source_target_pairs={{1,0},{2,1},{3,2},{4,3},{5,4},{6,5},{7,6},{8,7},{9,8},{10,9},{11,1... | collective-permute-start | bytes 786440 | tf_op jit(solution)/shard_map/ppermute | solution.py:18
  79.1 3.5 %copy-start.1 = (bf16[1,128,2048]{1,2,0:T(8,128)(2,1)S(1)}, bf16[1,128,2048]{1,2,0:T(8,128)(2,1)}, u32[]{:S(2)}) copy-start(bf16[1,128,2048]{1,2,0:T(8,128)(2,1)} %copy.77) | copy-start | bytes 1572868
  82.6 4.2 %copy-start.2 = (f32[128,4,128]{0,2,1:T(8,128)S(1)}, f32[128,4,128]{0,2,1:T(8,128)}, u32[]{:S(2)}) copy-start(f32[128,4,128]{0,2,1:T(8,128)} %get-tuple-element.13) | copy-start | bytes 786436
  84.9 43.0 %collective-permute-start.6 = (f32[128,512]{1,0:T(8,128)}, f32[128,512]{1,0:T(8,128)}, u32[]{:S(2)}, u32[]{:S(2)}) collective-permute-start(f32[128,512]{1,0:T(8,128)} %copy.47), channel_id=1, source_target_pairs={{1,0},{2,1},{3,2},{4,3},{5,4},{6,5},{7,6},{8,7},{9,8},{10,9},{11,1... | collective-permute-start | bytes 786440 | tf_op jit(solution)/shard_map/ppermute | solution.py:18
  126.0 16.8 %collective-permute-start.9 = (f32[128,512]{1,0:T(8,128)}, f32[128,512]{1,0:T(8,128)}, u32[]{:S(2)}, u32[]{:S(2)}) collective-permute-start(f32[128,512]{1,0:T(8,128)} %add.51), channel_id=1, source_target_pairs={{1,0},{2,1},{3,2},{4,3},{5,4},{6,5},{7,6},{8,7},{9,8},{10,9},{11,1... | collective-permute-start | bytes 786440 | tf_op jit(solution)/shard_map/ppermute | solution.py:18
  129.7 14.8 %collective-permute-start.7 = (f32[128,512]{1,0:T(8,128)}, f32[128,512]{1,0:T(8,128)}, u32[]{:S(2)}, u32[]{:S(2)}) collective-permute-start(f32[128,512]{1,0:T(8,128)} %add.49), channel_id=1, source_target_pairs={{1,0},{2,1},{3,2},{4,3},{5,4},{6,5},{7,6},{8,7},{9,8},{10,9},{11,1... | collective-permute-start | bytes 786440 | tf_op jit(solution)/shard_map/ppermute | solution.py:18
where the time goes:
time: 149 us; the launch traced here: 148 us
  starting transfers between devices  60.9 us (41%)
  waiting for transfers between devices  37.9 us (25%)
  local copies, waits for them, and re-layouts  23.2 us (16%)
  matrix products  13.4 us (9%)
  other arithmetic  11.3 us (8%)
    ppermute x10, starting transfers between devices, from_behind(): lax.ppermute(value, axis, [(source, source + steps) for source in range(l...  50.2 us
    ppermute x10, waiting for transfers between devices, from_behind(): lax.ppermute(value, axis, [(source, source + steps) for source in range(l...  37.9 us
    all_to_all x1, starting transfers between devices, regroup(): lax.all_to_all(packed, 'dp', split_axis=0, concat_axis=0, tiled=True)  10.7 us
    unnamed x26, local copies, waits for them, and re-layouts  6.37 us
    slice x8, local copies, waits for them, and re-layouts, term_rows(): return terms[start:start + block_len]  5.76 us
    dot_general x1, matrix products, backward_part(): jnp.einsum('qkgd,nkd->kgqn', grad_heads, value_heads, preferred_element_t...  3.45 us
    dot_general x1, matrix products, forward_part(): jnp.einsum('kgqn,nkd->qkgd', weights_low, value_heads, preferred_element_...  3.1 us
  transfers between devices with their start and end apart: 11, of which 2 were waited for; matrix products, arithmetic and copies ran while one was open for 25% of the time, Pallas kernels for 0%

commit v1 on v0

v1 whole, which is shorter than its diff:
```python
import functools
import math

import jax
import jax.numpy as jnp
from jax import lax
from jax.experimental import pallas as pl
from jax.experimental.pallas import tpu as pltpu
from jax.sharding import PartitionSpec as P

HEAD = 128
KV = 4
GROUP = 4
TOK = 128
WIDE = GROUP * HEAD
MESH = pl.DeviceIdType.MESH
NT = (((1,), (1,)), ((), ()))
SCALE = 1.0 / math.sqrt(HEAD)
F32 = jnp.float32
BF16 = jnp.bfloat16


def kernel(n_dp, n_ctx, q_hbm, k_hbm, v_hbm, g_hbm, seg_hbm, home_ref,
           routed, dq_hbm, dk_ref, dv_ref,
           q_s, g_s, kvx, kv1, segx, seg1, bias, sel, pk, dq_s,
           gs_out, gs_in, gz_out, gz_in, acc,
           in_sem, kv_sem, seg_send, seg_recv, f_send, f_recv, s_send, s_recv,
           a_send, a_recv, own_sem, dq_sem, gs_send, gs_recv, gz_send, gz_recv):
    dp = lax.axis_index("dp")
    ctx = lax.axis_index("ctx")
    core = lax.rem(ctx, 2)
    sib = ctx + 1 - 2 * core
    up = lax.rem(ctx + 2, n_ctx)
    down = lax.rem(ctx + n_ctx - 2, n_ctx)

    def remote(src, dst, send, recv, **where):
        return pltpu.make_async_remote_copy(
            src_ref=src, dst_ref=dst, send_sem=send, recv_sem=recv,
            device_id=where, device_id_type=MESH)

    barrier = pltpu.get_barrier_semaphore()
    pl.semaphore_signal(barrier, inc=1, device_id={"ctx": sib}, device_id_type=MESH)
    pl.semaphore_signal(barrier, inc=1, device_id={"ctx": up}, device_id_type=MESH)
    pl.semaphore_signal(barrier, inc=1, device_id={"ctx": down}, device_id_type=MESH)
    for r in range(1, n_dp):
        pl.semaphore_signal(barrier, inc=1, device_id={"dp": lax.rem(dp + r, n_dp)},
                            device_id_type=MESH)

    seg_load = pltpu.make_async_copy(seg_hbm, segx.at[0], in_sem.at[8])
    seg_load.start()
    kv_loads = []
    for h in range(KV):
        cols = pl.ds(h * HEAD, HEAD)
        kv_loads.append((
            pltpu.make_async_copy(k_hbm.at[:, cols], kvx.at[0, h, 0], kv_sem.at[h, 0]),
            pltpu.make_async_copy(v_hbm.at[:, cols], kvx.at[0, h, 1], kv_sem.at[h, 1])))
        for load in kv_loads[-1]:
            load.start()
    qg_loads = []
    for h in range(KV):
        cols = pl.ds(h * WIDE, WIDE)
        qg_loads.append(pltpu.make_async_copy(q_hbm.at[:, cols], q_s.at[h], in_sem.at[h]))
        qg_loads.append(pltpu.make_async_copy(g_hbm.at[:, cols], g_s.at[h], in_sem.at[4 + h]))
    for load in qg_loads:
        load.start()
    seg_load.wait()
    for pair in kv_loads:
        for load in pair:
            load.wait()
    pl.semaphore_wait(barrier, n_dp + 2)

    def seg_copy():
        return remote(segx.at[0], segx.at[1], seg_send.at[0], seg_recv.at[0], ctx=up)

    def seg_pass():
        return remote(segx.at[core], seg1, seg_send.at[1], seg_recv.at[1], ctx=sib)

    def fetch(h):
        return remote(kvx.at[0, h], kvx.at[1, h], f_send.at[h], f_recv.at[h], ctx=up)

    def sib_pass(h):
        return remote(kvx.at[core, h], kv1.at[h], s_send.at[h], s_recv.at[h], ctx=sib)

    def a2a(h, r):
        to = lax.rem(dp + r, n_dp)
        return remote(pk.at[h, to], routed.at[dp, :, pl.ds(pl.multiple_of(h * WIDE, WIDE), WIDE)],
                      a_send.at[h, r], a_recv.at[h, r], dp=to)

    def a2a_own(h):
        return pltpu.make_async_copy(
            pk.at[h, dp], routed.at[dp, :, pl.ds(pl.multiple_of(h * WIDE, WIDE), WIDE)],
            own_sem.at[h])

    def dq_store(h):
        return pltpu.make_async_copy(
            dq_s.at[h], dq_hbm.at[:, pl.ds(pl.multiple_of(h * WIDE, WIDE), WIDE)], dq_sem.at[h])

    def gs_copy(h):
        return remote(gs_out.at[h], gs_in.at[h], gs_send.at[h], gs_recv.at[h], ctx=sib)

    def gz_copy(h):
        return remote(gz_out.at[h], gz_in.at[h], gz_send.at[h], gz_recv.at[h], ctx=down)

    seg_copy().start()
    for h in range(KV):
        fetch(h).start()
    for load in qg_loads:
        load.wait()

    grow = lax.broadcasted_iota(jnp.int32, (16, TOK), 0)
    gcol = lax.broadcasted_iota(jnp.int32, (16, TOK), 1)
    expand = (grow == gcol // 8).astype(BF16)
    home_b = jnp.broadcast_to(home_ref[...].astype(F32), (8, 16)).astype(BF16)
    home_row = jnp.dot(home_b, expand, preferred_element_type=F32)[0:1, :]
    home_sq = jnp.broadcast_to(home_row, (TOK, TOK))
    sq_r = lax.broadcasted_iota(jnp.int32, (TOK, TOK), 0)
    sq_c = lax.broadcasted_iota(jnp.int32, (TOK, TOK), 1)
    same = (home_sq.T == home_sq) & (sq_r // 8 < sq_c // 8)
    slot_row = jnp.sum(jnp.where(same, 0.125, 0.0), axis=0, keepdims=True)
    s_r = lax.broadcasted_iota(jnp.int32, (n_dp * 16, TOK), 0)
    s_c = lax.broadcasted_iota(jnp.int32, (n_dp * 16, TOK), 1)
    pick = ((s_r // 16).astype(F32) == home_row) & ((s_r // 8 % 2).astype(F32) == slot_row)
    pick = pick & (s_r % 8 == s_c % 8)
    sel[...] = jnp.where(pick, 1.0, 0.0).astype(BF16)

    seg_copy().wait_recv()
    seg_pass().start()
    seg_pass().wait_recv()
    own_row = segx[0].astype(F32)

    def seg_equal(row):
        return jnp.broadcast_to(row.astype(F32), (TOK, TOK)).T == own_row

    low = -1e30
    bias[0:TOK, :] = jnp.where(seg_equal(segx[1]) & (ctx >= 2), 0.0, low)
    bias[TOK:2 * TOK, :] = jnp.where(seg_equal(seg1[...]) & (ctx >= 1), 0.0, low)
    bias[2 * TOK:, :] = jnp.where(seg_equal(segx[0]) & (sq_r <= sq_c), 0.0, low)

    def step(h, carry):
        fetch(h).wait_recv()
        sib_pass(h).start()
        sib_pass(h).wait_recv()
        keys = jnp.concatenate([kvx[1, h, 0], kv1[h, 0], kvx[0, h, 0]], axis=0)
        vals = jnp.concatenate([kvx[1, h, 1], kv1[h, 1], kvx[0, h, 1]], axis=0)
        qs = jnp.concatenate([q_s[h, :, g * HEAD:(g + 1) * HEAD] for g in range(GROUP)], axis=0)
        gs = jnp.concatenate([g_s[h, :, g * HEAD:(g + 1) * HEAD] for g in range(GROUP)], axis=0)
        scores = lax.dot_general(keys, qs, NT, preferred_element_type=F32)
        parts, lows = [], []
        for g in range(GROUP):
            s = scores[:, g * HEAD:(g + 1) * HEAD] * SCALE + bias[...]
            p = jnp.exp(s - jnp.max(s, axis=0, keepdims=True))
            w = p * (1.0 / jnp.sum(p, axis=0, keepdims=True))
            parts.append(w)
            lows.append(w.astype(BF16))
        low_all = jnp.concatenate(lows, axis=1)
        att = jnp.dot(vals.T, low_all, preferred_element_type=F32).astype(BF16)
        for g in range(GROUP):
            packed = lax.dot_general(sel[...], att[:, g * HEAD:(g + 1) * HEAD], NT,
                                     preferred_element_type=F32)
            pk[h, :, :, g * HEAD:(g + 1) * HEAD] = packed.astype(BF16).reshape(n_dp, 16, HEAD)
        for r in range(1, n_dp):
            a2a(h, r).start()
        a2a_own(h).start()

        gw = lax.dot_general(vals, gs, NT, preferred_element_type=F32)
        scaled = []
        for g in range(GROUP):
            gwg = gw[:, g * HEAD:(g + 1) * HEAD]
            delta = jnp.sum(lows[g].astype(F32) * gwg, axis=0, keepdims=True)
            scaled.append((parts[g] * (gwg - delta) * SCALE).astype(BF16))
        ds = jnp.concatenate(scaled, axis=1)
        dk = jnp.dot(ds, qs, preferred_element_type=F32)
        dv = jnp.dot(low_all, gs, preferred_element_type=F32)
        gs_out[h, 0] = dk[TOK:2 * TOK].astype(BF16)
        gs_out[h, 1] = dv[TOK:2 * TOK].astype(BF16)
        gs_copy(h).start()
        dqt = jnp.dot(keys.T, ds, preferred_element_type=F32)
        for g in range(GROUP):
            dq_s[h, :, g * HEAD:(g + 1) * HEAD] = dqt[:, g * HEAD:(g + 1) * HEAD].T.astype(BF16)
        dq_store(h).start()
        gs_copy(h).wait_recv()
        for i, term in ((0, dk), (1, dv)):
            other = gs_in[h, i].astype(F32)
            zero = jnp.zeros_like(other)
            gz_out[h, i] = (term[:TOK] + jnp.where(core == 1, other, zero)).astype(BF16)
            acc[h, i] = term[2 * TOK:] + jnp.where(core == 0, other, zero)
        gz_copy(h).start()
        return carry

    lax.fori_loop(0, KV, step, 0)

    for h in range(KV):
        gz_copy(h).wait_recv()
        cols = slice(h * HEAD, (h + 1) * HEAD)
        dk_ref[:, cols] = (acc[h, 0] + gz_in[h, 0].astype(F32)).astype(BF16)
        dv_ref[:, cols] = (acc[h, 1] + gz_in[h, 1].astype(F32)).astype(BF16)

    seg_copy().wait_send()
    seg_pass().wait_send()

    def drain(h, carry):
        fetch(h).wait_send()
        sib_pass(h).wait_send()
        gs_copy(h).wait_send()
        gz_copy(h).wait_send()
        dq_store(h).wait()
        a2a_own(h).wait()
        for r in range(1, n_dp):
            a2a(h, r).wait_send()
            a2a(h, r).wait_recv()
        return carry

    lax.fori_loop(0, KV, drain, 0)


def on_device(n_dp, n_ctx, query_rows, key_rows, value_rows, out_grad, segment_ids, home_rows):
    any_space = pl.BlockSpec(memory_space=pl.ANY)
    vmem = pl.BlockSpec(memory_space=pltpu.VMEM)
    dma = pltpu.SemaphoreType.DMA
    routed, dq, dk, dv = pl.pallas_call(
        functools.partial(kernel, n_dp, n_ctx),
        out_shape=(
            jax.ShapeDtypeStruct((n_dp, 16, KV * WIDE), BF16),
            jax.ShapeDtypeStruct((TOK, KV * WIDE), BF16),
            jax.ShapeDtypeStruct((TOK, KV * HEAD), BF16),
            jax.ShapeDtypeStruct((TOK, KV * HEAD), BF16),
        ),
        in_specs=[any_space] * 5 + [vmem],
        out_specs=(any_space, any_space, vmem, vmem),
        scratch_shapes=[
            pltpu.VMEM((KV, TOK, WIDE), BF16),
            pltpu.VMEM((KV, TOK, WIDE), BF16),
            pltpu.VMEM((2, KV, 2, TOK, HEAD), BF16),
            pltpu.VMEM((KV, 2, TOK, HEAD), BF16),
            pltpu.VMEM((2, 1, TOK), jnp.int32),
            pltpu.VMEM((1, TOK), jnp.int32),
            pltpu.VMEM((3 * TOK, TOK), F32),
            pltpu.VMEM((n_dp * 16, TOK), BF16),
            pltpu.VMEM((KV, n_dp, 16, WIDE), BF16),
            pltpu.VMEM((KV, TOK, WIDE), BF16),
            pltpu.VMEM((KV, 2, TOK, HEAD), BF16),
            pltpu.VMEM((KV, 2, TOK, HEAD), BF16),
            pltpu.VMEM((KV, 2, TOK, HEAD), BF16),
            pltpu.VMEM((KV, 2, TOK, HEAD), BF16),
            pltpu.VMEM((KV, 2, TOK, HEAD), F32),
            dma((9,)), dma((KV, 2)), dma((2,)), dma((2,)),
            dma((KV,)), dma((KV,)), dma((KV,)), dma((KV,)),
            dma((KV, n_dp)), dma((KV, n_dp)), dma((KV,)), dma((KV,)),
            dma((KV,)), dma((KV,)), dma((KV,)), dma((KV,)),
        ],
        compiler_params=pltpu.CompilerParams(collective_id=0, has_side_effects=True),
        name="fused_attention",
    )(query_rows[0], key_rows[0], value_rows[0], out_grad[0], segment_ids, home_rows)
    return (routed.reshape(1, 1, n_dp, 2, 8, KV * WIDE), dq[None], dk[None], dv[None])


def solution(mesh):
    n_dp, n_ctx = mesh.shape["dp"], mesh.shape["ctx"]
    rows = P("dp", "ctx", None)
    return jax.shard_map(
        functools.partial(on_device, n_dp, n_ctx),
        mesh=mesh,
        in_specs=(rows, rows, rows, rows, P("dp", "ctx"), P("dp", "ctx")),
        out_specs=(P("dp", "ctx", None, None, None, None), rows, rows, rows),
        check_vma=False,
    )
```

time: 149 us -> 87.2 us (0.59)
  the two profiles are of different devices: /device:TPU:163 before, /device:TPU:1 now
where the time goes in v1:
time: 87.2 us; the launch traced here: 87 us
  Pallas kernels  81.4 us (93%)
  local copies, waits for them, and re-layouts  4.99 us (6%)
    pallas_call x1, Pallas kernels, on_device(): pl.pallas_call(functools.partial(kernel, n_dp, n_ctx), out_shape=(jax.Sha...  81.4 us
    unnamed x10, local copies, waits for them, and re-layouts  4.99 us

profile of v1, /device:TPU:1, one launch (start us, length us, event | category | flops | bytes accessed | tf_op | source)
XLA Modules:
  0.0 87.0 jit_solution(5377091192560349709)
XLA Ops:
  0.6 81.4 %fused_attention.1 = (bf16[16,16,2048]{2,1,0:T(8,128)(2,1)}, bf16[128,2048]{1,0:T(8,128)(2,1)}, bf16[128,512]{1,0:T(8,128)(2,1)}, bf16[128,512]{1,0:T(8,128)(2,1)}) custom-call(bf16[128,2048]{1,0:T(8,128)(2,1)} %bitcast.9, bf16[128,512]{1,0:T(8,128)(2,1)} %bitcast.12, bf16[128,512]{1,0:T(8,128)(2,1)} %bitcast.13, bf16[128,2048]{1,0:T(8,128)(2,1)} %bitcast.10, ...), custom_call_target="tpu_custom_call" | custom-call | tf_op jit(solution)/shard_map/fused_attention/pallas_call | solution.py:220
  82.0 0.0 copy-start
  82.0 2.4 %copy.14 = bf16[1,1,16,2,8,2048]{5,4,3,2,1,0:T(8,128)(2,1)} copy(bf16[1,1,16,2,8,2048]{5,4,3,2,1,0:T(8,128)(2,1)} %bitcast.8) | data formatting | bytes 2097152
  84.4 0.0 copy-done
  84.4 0.0 copy-start.2
  84.4 0.8 copy.15
  85.2 0.2 copy-done.2
  85.4 0.0 copy-start.1
  85.4 0.7 copy.16
  86.1 0.3 copy-done.1
  86.4 0.7 copy.17
Async XLA Ops:
  82.0 2.4 %copy-start = (bf16[128,2048]{1,0:T(8,128)(2,1)S(1)}, bf16[128,2048]{1,0:T(8,128)(2,1)}, u32[]{:S(2)}) copy-start(bf16[128,2048]{1,0:T(8,128)(2,1)} %get-tuple-element.9) | copy-start | bytes 1572868
  84.4 1.0 %copy-start.2 = (bf16[128,512]{1,0:T(8,128)(2,1)S(1)}, bf16[128,512]{1,0:T(8,128)(2,1)}, u32[]{:S(2)}) copy-start(bf16[128,512]{1,0:T(8,128)(2,1)} %get-tuple-element.10) | copy-start | bytes 393220
  85.4 1.0 %copy-start.1 = (bf16[128,512]{1,0:T(8,128)(2,1)S(1)}, bf16[128,512]{1,0:T(8,128)(2,1)}, u32[]{:S(2)}) copy-start(bf16[128,512]{1,0:T(8,128)(2,1)} %get-tuple-element.11) | copy-start | bytes 393220

commit v2 on v1

--- a/solution.py
+++ b/solution.py
@@ -25,10 +25,12 @@
            q_s, g_s, kvx, kv1, segx, seg1, bias, sel, pk, dq_s,
            gs_out, gs_in, gz_out, gz_in, acc,
            in_sem, kv_sem, seg_send, seg_recv, f_send, f_recv, s_send, s_recv,
-           a_send, a_recv, own_sem, dq_sem, gs_send, gs_recv, gz_send, gz_recv):
+           a_send, a_recv, own_sem, dq_sem, gs_send, gs_recv, gz_send, gz_recv, met):
     dp = lax.axis_index("dp")
     ctx = lax.axis_index("ctx")
     core = lax.rem(ctx, 2)
+    first = lax.rem(ctx // 2, 3)
+    ahead = jnp.where(lax.rem(dp, 4) < 2, 2, 4)
     sib = ctx + 1 - 2 * core
     up = lax.rem(ctx + 2, n_ctx)
     down = lax.rem(ctx + n_ctx - 2, n_ctx)
@@ -40,11 +42,11 @@
 
     barrier = pltpu.get_barrier_semaphore()
     pl.semaphore_signal(barrier, inc=1, device_id={"ctx": sib}, device_id_type=MESH)
-    pl.semaphore_signal(barrier, inc=1, device_id={"ctx": up}, device_id_type=MESH)
     pl.semaphore_signal(barrier, inc=1, device_id={"ctx": down}, device_id_type=MESH)
-    for r in range(1, n_dp):
-        pl.semaphore_signal(barrier, inc=1, device_id={"dp": lax.rem(dp + r, n_dp)},
-                            device_id_type=MESH)
+    partners = []
+    for bit in range(n_dp.bit_length() - 1):
+        partners.append(dp + (1 << bit) - (2 << bit) * lax.rem(dp // (1 << bit), 2))
+        pl.semaphore_signal(barrier, inc=1, device_id={"dp": partners[-1]}, device_id_type=MESH)
 
     seg_load = pltpu.make_async_copy(seg_hbm, segx.at[0], in_sem.at[8])
     seg_load.start()
@@ -67,7 +69,7 @@
     for pair in kv_loads:
         for load in pair:
             load.wait()
-    pl.semaphore_wait(barrier, n_dp + 2)
+    pl.semaphore_wait(barrier, 2 + len(partners))
 
     def seg_copy():
         return remote(segx.at[0], segx.at[1], seg_send.at[0], seg_recv.at[0], ctx=up)
@@ -103,7 +105,12 @@
 
     seg_copy().start()
     for h in range(KV):
-        fetch(h).start()
+        @pl.when(h < ahead)
+        def _(h=h):
+            fetch(h).start()
+    for i, partner in enumerate(partners):
+        pl.semaphore_signal(met.at[i], inc=1, device_id={"dp": partner}, device_id_type=MESH)
+        pl.semaphore_wait(met.at[i], 1)
     for load in qg_loads:
         load.wait()
 
@@ -125,6 +132,14 @@
 
     seg_copy().wait_recv()
     seg_pass().start()
+    fetch(0).wait_recv()
+    sib_pass(0).start()
+
+    for h in range(1, KV):
+        @pl.when(h >= ahead)
+        def _(h=h):
+            fetch(h).start()
+
     seg_pass().wait_recv()
     own_row = segx[0].astype(F32)
 
@@ -137,8 +152,6 @@
     bias[2 * TOK:, :] = jnp.where(seg_equal(segx[0]) & (sq_r <= sq_c), 0.0, low)
 
     def step(h, carry):
-        fetch(h).wait_recv()
-        sib_pass(h).start()
         sib_pass(h).wait_recv()
         keys = jnp.concatenate([kvx[1, h, 0], kv1[h, 0], kvx[0, h, 0]], axis=0)
         vals = jnp.concatenate([kvx[1, h, 1], kv1[h, 1], kvx[0, h, 1]], axis=0)
@@ -178,16 +191,32 @@
         for g in range(GROUP):
             dq_s[h, :, g * HEAD:(g + 1) * HEAD] = dqt[:, g * HEAD:(g + 1) * HEAD].T.astype(BF16)
         dq_store(h).start()
+
+        @pl.when(h < KV - 1)
+        def _():
+            fetch(h + 1).wait_recv()
+            sib_pass(h + 1).start()
+
         gs_copy(h).wait_recv()
         for i, term in ((0, dk), (1, dv)):
             other = gs_in[h, i].astype(F32)
             zero = jnp.zeros_like(other)
             gz_out[h, i] = (term[:TOK] + jnp.where(core == 1, other, zero)).astype(BF16)
             acc[h, i] = term[2 * TOK:] + jnp.where(core == 0, other, zero)
-        gz_copy(h).start()
+
+        @pl.when(first != 0)
+        def _():
+            gz_copy(h).start()
+
         return carry
 
     lax.fori_loop(0, KV, step, 0)
+
+    @pl.when(first == 0)
+    def _():
+        for h in range(KV):
+            gz_copy(h).start()
+
 
     for h in range(KV):
         gz_copy(h).wait_recv()
@@ -213,7 +242,17 @@
     lax.fori_loop(0, KV, drain, 0)
 
 
+def settle(*refs):
+    done = refs[8]
+    copies = [pltpu.make_async_copy(refs[i], refs[4 + i], done.at[i]) for i in range(4)]
+    for copy in copies:
+        copy.start()
+    for copy in copies:
+        copy.wait()
+
+
 def on_device(n_dp, n_ctx, query_rows, key_rows, value_rows, out_grad, segment_ids, home_rows):
+    hbm = pl.BlockSpec(memory_space=pltpu.HBM)
     any_space = pl.BlockSpec(memory_space=pl.ANY)
     vmem = pl.BlockSpec(memory_space=pltpu.VMEM)
     dma = pltpu.SemaphoreType.DMA
@@ -225,7 +264,7 @@
             jax.ShapeDtypeStruct((TOK, KV * HEAD), BF16),
             jax.ShapeDtypeStruct((TOK, KV * HEAD), BF16),
         ),
-        in_specs=[any_space] * 5 + [vmem],
+        in_specs=[hbm] * 5 + [vmem],
         out_specs=(any_space, any_space, vmem, vmem),
         scratch_shapes=[
             pltpu.VMEM((KV, TOK, WIDE), BF16),
@@ -247,10 +286,21 @@
             dma((KV,)), dma((KV,)), dma((KV,)), dma((KV,)),
             dma((KV, n_dp)), dma((KV, n_dp)), dma((KV,)), dma((KV,)),
             dma((KV,)), dma((KV,)), dma((KV,)), dma((KV,)),
+            pltpu.SemaphoreType.REGULAR((4,)),
         ],
-        compiler_params=pltpu.CompilerParams(collective_id=0, has_side_effects=True),
+        compiler_params=pltpu.CompilerParams(collective_id=0, has_side_effects=True,
+                                             vmem_limit_bytes=24 * 1024 * 1024),
         name="fused_attention",
     )(query_rows[0], key_rows[0], value_rows[0], out_grad[0], segment_ids, home_rows)
+    routed, dq, dk, dv = pl.pallas_call(
+        settle,
+        out_shape=tuple(jax.ShapeDtypeStruct(a.shape, a.dtype) for a in (routed, dq, dk, dv)),
+        in_specs=[any_space] * 4,
+        out_specs=(hbm,) * 4,
+        scratch_shapes=[dma((4,))],
+        compiler_params=pltpu.CompilerParams(vmem_limit_bytes=1024 * 1024),
+        name="settle",
+    )(routed, dq, dk, dv)
     return (routed.reshape(1, 1, n_dp, 2, 8, KV * WIDE), dq[None], dk[None], dv[None])
 
 

time: 87.2 us -> 79.4 us (0.911)
  the two profiles are of different devices: /device:TPU:1 before, /device:TPU:129 now
where the time goes in v2:
time: 79.4 us; the launch traced here: 79.1 us
  Pallas kernels  73.9 us (93%)
  local copies, waits for them, and re-layouts  4.55 us (6%)
    pallas_call x1, Pallas kernels, on_device(): pl.pallas_call(functools.partial(kernel, n_dp, n_ctx), out_shape=(jax.Sha...  72.6 us
    unnamed x12, local copies, waits for them, and re-layouts  4.55 us

profile of v2, /device:TPU:129, one launch (start us, length us, event | category | flops | bytes accessed | tf_op | source)
XLA Modules:
  0.0 79.1 jit_solution(7124566397145534824)
XLA Ops:
  0.6 0.0 copy-start.4
  0.6 0.0 copy-start.5
  0.7 0.6 copy-done.4
  1.3 0.0 copy-done.5
  1.3 0.0 copy-start
  1.3 1.0 %copy-done = bf16[1,128,2048]{2,1,0:T(8,128)(2,1)S(1)} copy-done((bf16[1,128,2048]{2,1,0:T(8,128)(2,1)S(1)}, bf16[1,128,2048]{2,1,0:T(8,128)(2,1)}, u32[]{:S(2)}) %copy-start) | copy-done | bytes 524312
  2.3 0.0 copy-start.1
  2.3 1.0 %copy-done.1 = bf16[1,128,2048]{2,1,0:T(8,128)(2,1)S(1)} copy-done((bf16[1,128,2048]{2,1,0:T(8,128)(2,1)S(1)}, bf16[1,128,2048]{2,1,0:T(8,128)(2,1)}, u32[]{:S(2)}) %copy-start.1) | copy-done | bytes 524312
  3.4 0.0 copy-start.2
  3.4 0.9 %copy-done.2 = bf16[1,128,512]{2,1,0:T(8,128)(2,1)S(1)} copy-done((bf16[1,128,512]{2,1,0:T(8,128)(2,1)S(1)}, bf16[1,128,512]{2,1,0:T(8,128)(2,1)}, u32[]{:S(2)}) %copy-start.2) | copy-done | bytes 131096
  4.3 0.0 copy-start.3
  4.3 0.9 %copy-done.3 = bf16[1,128,512]{2,1,0:T(8,128)(2,1)S(1)} copy-done((bf16[1,128,512]{2,1,0:T(8,128)(2,1)S(1)}, bf16[1,128,512]{2,1,0:T(8,128)(2,1)}, u32[]{:S(2)}) %copy-start.3) | copy-done | bytes 131096
  5.2 72.6 %fused_attention.1 = (bf16[16,16,2048]{2,1,0:T(8,128)(2,1)S(1)}, bf16[128,2048]{1,0:T(8,128)(2,1)S(1)}, bf16[128,512]{1,0:T(8,128)(2,1)S(1)}, bf16[128,512]{1,0:T(8,128)(2,1)S(1)}) custom-call(bf16[128,2048]{1,0:T(8,128)(2,1)S(1)} %bitcast.8, bf16[128,512]{1,0:T(8,128)(2,1)S(1)} %bitcast.10, bf16[128,512]{1,0:T(8,128)(2,1)S(1)} %bitcast.11, ...), custom_call_target="tpu_custom_call" | custom-call | tf_op jit(solution)/shard_map/fused_attention/pallas_call | solution.py:259
  77.8 1.3 %settle.1 = (bf16[16,16,2048]{2,1,0:T(8,128)(2,1)}, bf16[128,2048]{1,0:T(8,128)(2,1)}, bf16[128,512]{1,0:T(8,128)(2,1)}, bf16[128,512]{1,0:T(8,128)(2,1)}) custom-call(bf16[16,16,2048]{2,1,0:T(8,128)(2,1)S(1)} %get-tuple-element.12.refs_0_, bf16[128,2048]{1,0:T(8,128)(2,1)S(1)} %get-tuple-element.13.refs_1_, bf16[128,512]{1,0:T(8,128)(2,1)S(1)} %get-tuple-element.14.refs_2_, ...), custom_call_target="tpu_custom_call" | custom-call | tf_op jit(solution)/shard_map/settle/pallas_call | solution.py:295
Async XLA Ops:
  0.6 0.7 copy-start.4
  0.6 0.7 copy-start.5
  1.3 1.0 %copy-start = (bf16[1,128,2048]{2,1,0:T(8,128)(2,1)S(1)}, bf16[1,128,2048]{2,1,0:T(8,128)(2,1)}, u32[]{:S(2)}) copy-start(bf16[1,128,2048]{2,1,0:T(8,128)(2,1)} %param.6) | copy-start | bytes 1572868
  2.3 1.0 %copy-start.1 = (bf16[1,128,2048]{2,1,0:T(8,128)(2,1)S(1)}, bf16[1,128,2048]{2,1,0:T(8,128)(2,1)}, u32[]{:S(2)}) copy-start(bf16[1,128,2048]{2,1,0:T(8,128)(2,1)} %param.9) | copy-start | bytes 1572868
  3.4 0.9 %copy-start.2 = (bf16[1,128,512]{2,1,0:T(8,128)(2,1)S(1)}, bf16[1,128,512]{2,1,0:T(8,128)(2,1)}, u32[]{:S(2)}) copy-start(bf16[1,128,512]{2,1,0:T(8,128)(2,1)} %param.7) | copy-start | bytes 393220
  4.3 0.9 %copy-start.3 = (bf16[1,128,512]{2,1,0:T(8,128)(2,1)S(1)}, bf16[1,128,512]{2,1,0:T(8,128)(2,1)}, u32[]{:S(2)}) copy-start(bf16[1,128,512]{2,1,0:T(8,128)(2,1)} %param.8) | copy-start | bytes 393220

commit v3 on v2

--- a/solution.py
+++ b/solution.py
@@ -20,17 +20,17 @@
 BF16 = jnp.bfloat16
 
 
-def kernel(n_dp, n_ctx, q_hbm, k_hbm, v_hbm, g_hbm, seg_hbm, home_ref,
+def kernel(n_dp, n_ctx, q_hbm, k_hbm, v_hbm, g_hbm, seg_hbm, home_hbm,
            routed, dq_hbm, dk_ref, dv_ref,
-           q_s, g_s, kvx, kv1, segx, seg1, bias, sel, pk, dq_s,
+           home_s, q_s, g_s, kvx, kv1, segx, seg1, bias, sel, pk, dq_s,
            gs_out, gs_in, gz_out, gz_in, acc,
            in_sem, kv_sem, seg_send, seg_recv, f_send, f_recv, s_send, s_recv,
            a_send, a_recv, own_sem, dq_sem, gs_send, gs_recv, gz_send, gz_recv, met):
     dp = lax.axis_index("dp")
     ctx = lax.axis_index("ctx")
     core = lax.rem(ctx, 2)
-    first = lax.rem(ctx // 2, 3)
-    ahead = jnp.where(lax.rem(dp, 4) < 2, 2, 4)
+    first = jnp.where(lax.rem(dp, 4) < 2, 1, lax.rem(ctx // 2, 3))
+    ahead = jnp.where(lax.rem(dp, 4) < 2, 2 - lax.rem(dp, 4), 4)
     sib = ctx + 1 - 2 * core
     up = lax.rem(ctx + 2, n_ctx)
     down = lax.rem(ctx + n_ctx - 2, n_ctx)
@@ -50,6 +50,8 @@
 
     seg_load = pltpu.make_async_copy(seg_hbm, segx.at[0], in_sem.at[8])
     seg_load.start()
+    home_load = pltpu.make_async_copy(home_hbm, home_s, in_sem.at[9])
+    home_load.start()
     kv_loads = []
     for h in range(KV):
         cols = pl.ds(h * HEAD, HEAD)
@@ -66,6 +68,7 @@
     for load in qg_loads:
         load.start()
     seg_load.wait()
+    home_load.wait()
     for pair in kv_loads:
         for load in pair:
             load.wait()
@@ -117,7 +120,7 @@
     grow = lax.broadcasted_iota(jnp.int32, (16, TOK), 0)
     gcol = lax.broadcasted_iota(jnp.int32, (16, TOK), 1)
     expand = (grow == gcol // 8).astype(BF16)
-    home_b = jnp.broadcast_to(home_ref[...].astype(F32), (8, 16)).astype(BF16)
+    home_b = jnp.broadcast_to(home_s[...].astype(F32), (8, 16)).astype(BF16)
     home_row = jnp.dot(home_b, expand, preferred_element_type=F32)[0:1, :]
     home_sq = jnp.broadcast_to(home_row, (TOK, TOK))
     sq_r = lax.broadcasted_iota(jnp.int32, (TOK, TOK), 0)
@@ -264,9 +267,10 @@
             jax.ShapeDtypeStruct((TOK, KV * HEAD), BF16),
             jax.ShapeDtypeStruct((TOK, KV * HEAD), BF16),
         ),
-        in_specs=[hbm] * 5 + [vmem],
+        in_specs=[hbm] * 6,
         out_specs=(any_space, any_space, vmem, vmem),
         scratch_shapes=[
+            pltpu.VMEM((1, 16), jnp.int32),
             pltpu.VMEM((KV, TOK, WIDE), BF16),
             pltpu.VMEM((KV, TOK, WIDE), BF16),
             pltpu.VMEM((2, KV, 2, TOK, HEAD), BF16),
@@ -282,7 +286,7 @@
             pltpu.VMEM((KV, 2, TOK, HEAD), BF16),
             pltpu.VMEM((KV, 2, TOK, HEAD), BF16),
             pltpu.VMEM((KV, 2, TOK, HEAD), F32),
-            dma((9,)), dma((KV, 2)), dma((2,)), dma((2,)),
+            dma((10,)), dma((KV, 2)), dma((2,)), dma((2,)),
             dma((KV,)), dma((KV,)), dma((KV,)), dma((KV,)),
             dma((KV, n_dp)), dma((KV, n_dp)), dma((KV,)), dma((KV,)),
             dma((KV,)), dma((KV,)), dma((KV,)), dma((KV,)),
@@ -291,7 +295,8 @@
         compiler_params=pltpu.CompilerParams(collective_id=0, has_side_effects=True,
                                              vmem_limit_bytes=24 * 1024 * 1024),
         name="fused_attention",
-    )(query_rows[0], key_rows[0], value_rows[0], out_grad[0], segment_ids, home_rows)
+    )(*(pltpu.with_memory_space_constraint(a, pltpu.HBM) for a in (
+        query_rows[0], key_rows[0], value_rows[0], out_grad[0], segment_ids, home_rows)))
     routed, dq, dk, dv = pl.pallas_call(
         settle,
         out_shape=tuple(jax.ShapeDtypeStruct(a.shape, a.dtype) for a in (routed, dq, dk, dv)),

time: 79.4 us -> 73.9 us (0.931)
  local copies, waits for them, and re-layouts: 4.55 us -> 0 us
  Pallas kernels: 73.9 us -> 73.1 us
    unnamed x12 -> x0, local copies, waits for them, and re-layouts: 4.55 us -> none
    pallas_call x1, Pallas kernels: 72.6 us -> 71.8 us  [on_device(): pl.pallas_call(functools.partial(kernel, n_dp, n_ctx), out_shape=(jax.Sha...]
where the time goes in v3:
time: 73.9 us; the launch traced here: 73.7 us
  Pallas kernels  73.1 us (99%)
    pallas_call x1, Pallas kernels, on_device(): pl.pallas_call(functools.partial(kernel, n_dp, n_ctx), out_shape=(jax.Sha...  71.8 us

profile of v3, /device:TPU:129, one launch (start us, length us, event | category | flops | bytes accessed | tf_op | source)
XLA Modules:
  0.0 73.7 jit_solution(1892386213889991247)
XLA Ops:
  0.6 71.8 %fused_attention.1 = (bf16[16,16,2048]{2,1,0:T(8,128)(2,1)S(1)}, bf16[128,2048]{1,0:T(8,128)(2,1)S(1)}, bf16[128,512]{1,0:T(8,128)(2,1)S(1)}, bf16[128,512]{1,0:T(8,128)(2,1)S(1)}) custom-call(bf16[128,2048]{1,0:T(8,128)(2,1)} %bitcast.8, bf16[128,512]{1,0:T(8,128)(2,1)} %bitcast.10, bf16[128,512]{1,0:T(8,128)(2,1)} %bitcast.11, bf16[128,2048]{1,0:T(8,128)(2,1)} %bitcast.9, ...), custom_call_target="tpu_custom_call" | custom-call | tf_op jit(solution)/shard_map/fused_attention/pallas_call | solution.py:262
  72.4 1.3 %settle.1 = (bf16[16,16,2048]{2,1,0:T(8,128)(2,1)}, bf16[128,2048]{1,0:T(8,128)(2,1)}, bf16[128,512]{1,0:T(8,128)(2,1)}, bf16[128,512]{1,0:T(8,128)(2,1)}) custom-call(bf16[16,16,2048]{2,1,0:T(8,128)(2,1)S(1)} %get-tuple-element.12.refs_0_, bf16[128,2048]{1,0:T(8,128)(2,1)S(1)} %get-tuple-element.13.refs_1_, bf16[128,512]{1,0:T(8,128)(2,1)S(1)} %get-tuple-element.14.refs_2_, ...), custom_call_target="tpu_custom_call" | custom-call | tf_op jit(solution)/shard_map/settle/pallas_call | solution.py:300
